TPU v7x, 32 devices: a whole 2x2x4 slice. The times are simulated.
32 devices in a mesh: lon: 8 (over y, x, core), lat: 4 (over z).
Axes of the slice: x: 2, y: 2, z: 4, core: 2. Of those that a mesh axis runs over, the one named last changes fastest.
Arguments:
- latent: bfloat16 [4, 64, 128, 320], P(None, 'lat', 'lon'), may hold values from -28 to 28, as said below
- norm1_gain: float32 [320], replicated, may hold values from 0.1 to 1.9
- norm1_shift: float32 [320], replicated, may hold values from -3 to 3
- conv1_weight: bfloat16 [3, 3, 320, 320], replicated, may hold values from -0.109375 to 0.109375
- conv1_bias: float32 [320], replicated, may hold values from -3 to 3
- emb_shift: float32 [4, 320], replicated, may hold values from -4 to 4
- norm2_gain: float32 [320], replicated, may hold values from 0.1 to 1.9
- norm2_shift: float32 [320], replicated, may hold values from -3 to 3
- conv2_weight: bfloat16 [3, 3, 320, 320], replicated, may hold values from -0.109375 to 0.109375
- conv2_bias: float32 [320], replicated, may hold values from -3 to 3
Outputs:
- block_out: bfloat16 [4, 64, 128, 320], P(None, 'lat', 'lon')
Inputs may be any that keep to these rules, and one draw needn't show every extreme that they name: `latent`: Real-valued activations.
All inputs are finite; a program needn't handle non-finite values.
Results may differ from a plain program's by a relative error of at most 0.007.
Values may be sent and summed in bfloat16 or wider, within the bound.
No kernel may reach another device: no remote copies, remote signals or barrier semaphores. Data moves between devices by JAX's collectives and lax.ppermute only.
A program may use at most 64 MiB of HBM per device.

v0:
```python
import jax
import jax.numpy as jnp
from jax import lax
from jax.sharding import PartitionSpec as P

GROUPS = 32


def padded_2(array, sides, width, wrap):
    for axis, dim in sides:
        devices, length = (lax.axis_size(axis), array.shape[dim])
        up = [(i, (i + 1) % devices) for i in range(devices if wrap else devices - 1)]
        down = [(j, i) for i, j in up]
        last = lax.slice_in_dim(array, length - width, length, axis=dim)
        leading = lax.slice_in_dim(array, 0, width, axis=dim)
        before = lax.ppermute(last, axis, up)
        after = lax.ppermute(leading, axis, down)
        array = jnp.concatenate([before, array, after], axis=dim)
    return array


def from_behind(array, axis, by):
    devices = lax.axis_size(axis)
    return lax.ppermute(array, axis, [(i, (i + by) % devices) for i in range(devices)])


def group_stats(field, cell_count):
    frame_count = field.shape[0]
    grouped = field.reshape(frame_count, -1, GROUPS, field.shape[3] // GROUPS)
    summed, squares = lax.psum(
        (jnp.sum(grouped, axis=(1, 3)), jnp.sum(grouped * grouped, axis=(1, 3))), ("lon", "lat")
    )
    average = summed / cell_count
    variance = squares / cell_count - average * average
    return (average, lax.rsqrt(variance + 1e-05))


def activate(field, average, inverse, norm_gain, norm_shift):
    per_group = field.shape[3] // GROUPS
    per_mean = jnp.repeat(average, per_group, axis=1)[:, None, None, :]
    per_inverse = jnp.repeat(inverse, per_group, axis=1)[:, None, None, :]
    normed = (field - per_mean) * per_inverse * norm_gain + norm_shift
    return jax.nn.silu(normed).astype(jnp.bfloat16)


def sphere_pad(field):
    side_padded = padded_2(field, (("lon", 2),), 1, True)
    both_padded = padded_2(side_padded, (("lat", 1),), 1, False)
    north_row, south_row = from_behind(
        (side_padded[:, 0], side_padded[:, -1]), "lon", lax.axis_size("lon") // 2
    )
    lat_index = lax.axis_index("lat")
    first_row = jnp.where(lat_index == 0, north_row, both_padded[:, 0])
    final_row = jnp.where(lat_index == lax.axis_size("lat") - 1, south_row, both_padded[:, -1])
    return jnp.concatenate([first_row[:, None], both_padded[:, 1:-1], final_row[:, None]], axis=1)


def padded_input(source, cell_count, norm_gain, norm_shift):
    source_f = source.astype(jnp.float32)
    average, inverse = group_stats(source_f, cell_count)
    return sphere_pad(activate(source_f, average, inverse, norm_gain, norm_shift))


def convolve(padded, weight):
    return lax.conv_general_dilated(
        padded,
        weight,
        (1, 1),
        "VALID",
        dimension_numbers=("NHWC", "HWIO", "NHWC"),
        preferred_element_type=jnp.float32,
    )


def on_device(
    latent,
    norm1_gain,
    norm1_shift,
    conv1_weight,
    conv1_bias,
    emb_shift,
    norm2_gain,
    norm2_shift,
    conv2_weight,
    conv2_bias,
):
    per_group = latent.shape[3] // GROUPS
    cell_count = (
        latent.shape[1] * latent.shape[2] * lax.axis_size("lat") * lax.axis_size("lon") * per_group
    )
    first_padded = padded_input(latent, cell_count, norm1_gain, norm1_shift)
    hidden = convolve(first_padded, conv1_weight) + conv1_bias + emb_shift[:, None, None, :]
    hidden = hidden.astype(jnp.bfloat16)
    second_padded = padded_input(hidden, cell_count, norm2_gain, norm2_shift)
    branch = convolve(second_padded, conv2_weight) + conv2_bias
    return (latent.astype(jnp.float32) + branch).astype(jnp.bfloat16)


def solution(mesh):
    placed = (P(None, "lat", "lon", None), P(), P(), P(), P(), P(), P(), P(), P(), P())
    return jax.shard_map(
        on_device,
        mesh=mesh,
        in_specs=placed,
        out_specs=P(None, "lat", "lon", None),
        check_vma=False,
    )
```

profile of v0, /device:TPU:0, one launch (start us, length us, event | category | flops | bytes accessed | tf_op | source)
XLA Modules:
  0.0 154.9 jit_solution(12832509377845679093)
XLA Ops:
  0.0 2.1 %convert_reduce_fusion = (f32[4,320]{1,0:T(4,128)S(1)}, f32[4,320]{1,0:T(4,128)S(1)}) fusion(bf16[4,16,16,320]{3,2,1,0:T(8,128)(2,1)} %param.10), kind=kLoop, calls=%fused_computation.6 | loop fusion | flops 1308160 | bytes 665600 | tf_op jit(solution)/shard_map/reduce_sum | solution.py:31
  2.1 0.1 reduce_sum.47
  2.2 0.1 reduce_sum.53
  2.4 0.1 reduce_sum.51
  2.5 0.1 reduce_sum.54
  2.6 42.0 %all-reduce.1 = (f32[4,32]{1,0:T(4,128)S(1)}, f32[4,32]{1,0:T(4,128)S(1)}) all-reduce(f32[4,32]{1,0:T(4,128)S(1)} %reduce_sum.54, f32[4,32]{1,0:T(4,128)S(1)} %reduce_sum.51), channel_id=1, replica_groups=mesh['lon'=8,'lat'=4] {'lon','lat'}, use_global_device_ids=true, to_apply=%region_5.6 | all-reduce | flops 256 | bytes 2048 | tf_op jit(solution)/shard_map/psum | solution.py:30
  44.6 0.1 sub.26
  44.8 0.1 mul.59
  45.0 2.4 %fusion.18 = bf16[4,16,16,320]{3,0,2,1:T(4,128)(2,1)S(1)} fusion(f32[320]{0:T(512)} %param.12, f32[320]{0:T(512)} %param.11, f32[4,320]{1,0:T(4,128)S(1)} %mul.59, f32[4,320]{1,0:T(4,128)S(1)} %sub.26, bf16[4,16,16,320]{3,2,1,0:T(8,128)(2,1)} %param.10), kind=kLoop, calls=%fused_computation.32 | loop fusion | flops 3276800 | bytes 1323520 | tf_op jit(solution)/shard_map/convert_element_type | solution.py:43
  47.5 2.6 %collective-permute-start.1 = (bf16[4,16,1,320]{3,0,2,1:T(4,128)(2,1)S(1)}, bf16[4,16,1,320]{3,0,2,1:T(4,128)(2,1)S(1)}, u32[]{:S(2)}, u32[]{:S(2)}) collective-permute-start(bf16[4,16,1,320]{3,0,2,1:T(4,128)(2,1)S(1)} %get-tuple-element.18), channel_id=1, source_target_pairs={{4,0},{8,4},{12,8},{16,12},{20,16},{24,20},{28,24},{0,28},{5,1},{9... | collective-permute-start | bytes 122888 | tf_op jit(solution)/shard_map/ppermute | solution.py:17
  50.1 1.8 %collective-permute-done = bf16[4,16,1,320]{3,0,2,1:T(4,128)(2,1)S(1)} collective-permute-done((bf16[4,16,1,320]{3,0,2,1:T(4,128)(2,1)S(1)}, bf16[4,16,1,320]{3,0,2,1:T(4,128)(2,1)S(1)}, u32[]{:S(2)}, u32[]{:S(2)}) %collective-permute-start) | collective-permute-done | bytes 40992 | tf_op jit(solution)/shard_map/ppermute | solution.py:16
  51.9 0.1 pad_maximum_fusion.5
  52.0 2.3 %collective-permute-start.4 = (bf16[4,18,320]{2,0,1:T(4,128)(2,1)S(1)}, bf16[4,18,320]{2,0,1:T(4,128)(2,1)S(1)}, u32[]{:S(2)}, u32[]{:S(2)}) collective-permute-start(bf16[4,18,320]{2,0,1:T(4,128)(2,1)S(1)} %bitcast.78), channel_id=1, source_target_pairs={{0,16},{4,20},{8,24},{12,28},{16,0},{20,4},{24,8},{28,12},{1,17},{... | collective-permute-start | bytes 138248 | tf_op jit(solution)/shard_map/ppermute | solution.py:24
  54.3 1.3 collective-permute-start.5
  55.6 4.7 %collective-permute-start.3 = (bf16[4,1,18,320]{3,0,2,1:T(4,128)(2,1)S(1)}, bf16[4,1,18,320]{3,0,2,1:T(4,128)(2,1)S(1)}, u32[]{:S(2)}, u32[]{:S(2)}) collective-permute-start(bf16[4,1,18,320]{3,0,2,1:T(4,128)(2,1)S(1)} %get-tuple-element.14), channel_id=1, source_target_pairs={{0,1},{1,2},{2,3},{4,5},{5,6},{6,7},{8,9},{9,10},{10,11},{12,13},{... | collective-permute-start | bytes 138248 | tf_op jit(solution)/shard_map/ppermute | solution.py:16
  60.4 0.1 collective-permute-start.2
  60.5 4.1 %collective-permute-done.2 = bf16[4,18,320]{2,0,1:T(4,128)(2,1)S(1)} collective-permute-done((bf16[4,18,320]{2,0,1:T(4,128)(2,1)S(1)}, bf16[4,18,320]{2,0,1:T(4,128)(2,1)S(1)}, u32[]{:S(2)}, u32[]{:S(2)}) %collective-permute-start.2) | collective-permute-done | bytes 46112 | tf_op jit(solution)/shard_map/ppermute | solution.py:24
  64.6 0.9 maximum_bitcast_fusion.1
  65.6 0.5 pad
  66.1 0.3 slice.44
  66.4 1.0 fusion.5
  67.5 0.2 broadcast.25
  67.6 0.5 copy-done.7
  68.1 7.1 %fusion.30 = (f32[16,32,3,320]{3,1,2,0:T(8,128)S(1)}, f32[16,32,3,320]{3,1,2,0:T(8,128)}) fusion(f32[16,32,3,320]{3,0,2,1:T(8,128)S(1)} %bitcast.75, f32[320]{0:T(512)S(1)} %copy-done.7, bf16[3,3,320,320]{3,2,1,0:T(8,128)(2,1)S(1)} %copy-done, bf16[18,4,8,5,320]{4,1,3,2,0:T(4,128)(2,1)S(1)} %fusion.5, pred[32,3]{0,1:T(4,128)(4,1)S(1)} %copy-done.9), kind=kOutput, calls=%fused_computation.59 | convolution fusion | flops 2834104320 | bytes 9586016 | tf_op jit(solution)/shard_map/conv_general_dilated | solution.py:65
  75.2 1.4 copy.121
  76.6 0.1 slice_reduce_fusion
  76.7 0.1 reduce_sum.74
  76.8 0.1 reduce_sum.75
  76.9 3.0 %copy.119 = f32[16,32,3,320]{3,0,2,1:T(8,128)S(1)} copy(f32[16,32,3,320]{3,1,2,0:T(8,128)} %get-tuple-element.24) | data formatting | bytes 3932160 | tf_op jit(solution)/shard_map/convert_element_type | solution.py:59
  79.9 0.1 slice_reduce_fusion.1
  80.0 0.1 reduce_sum.59
  80.2 0.1 reduce_sum.72
  80.2 39.4 %all-reduce = (f32[4,32]{1,0:T(4,128)S(1)}, f32[4,32]{1,0:T(4,128)S(1)}) all-reduce(f32[4,32]{1,0:T(4,128)S(1)} %reduce_sum.75, f32[4,32]{1,0:T(4,128)S(1)} %reduce_sum.72), channel_id=1, replica_groups=mesh['lon'=8,'lat'=4] {'lon','lat'}, use_global_device_ids=true, to_apply=%region_11.12 | all-reduce | flops 256 | bytes 2048 | tf_op jit(solution)/shard_map/psum | solution.py:30
  119.7 0.1 sub.30
  119.9 0.1 mul.67
  120.1 0.2 broadcast.27
  120.3 0.2 broadcast.26
  120.4 1.3 copy-done.1
  121.7 1.8 %multiply_convert_fusion = bf16[16,32,3,320]{3,1,2,0:T(8,128)(2,1)S(1)} fusion(f32[16,32,3,320]{3,0,2,1:T(8,128)S(1)} %bitcast.65, f32[16,32,3,320]{3,1,2,0:T(8,128)S(1)} %copy-done.1, f32[16,32,3,320]{3,0,2,1:T(8,128)S(1)} %bitcast.66, f32[320]{0:T(512)S(1)} %copy-done.4, f32[320]{0:T(512)S(1)} %copy-done.5), kind=kLoop, calls=%fused_computation.14 | loop fusion | flops 4423680 | bytes 6883840 | tf_op jit(solution)/shard_map/convert_element_type | solution.py:43
  123.5 0.4 copy.123
  123.9 0.1 slice_bitcast_fusion
  124.1 2.6 %collective-permute-start.7 = (bf16[4,16,1,320]{3,1,2,0:T(8,128)(2,1)S(1)}, bf16[4,16,1,320]{3,1,2,0:T(8,128)(2,1)S(1)}, u32[]{:S(2)}, u32[]{:S(2)}) collective-permute-start(bf16[4,16,1,320]{3,1,2,0:T(8,128)(2,1)S(1)} %get-tuple-element.16), channel_id=1, source_target_pairs={{4,0},{8,4},{12,8},{16,12},{20,16},{24,20},{28,24},{0,28},{5,1},{9... | collective-permute-start | bytes 122888 | tf_op jit(solution)/shard_map/ppermute | solution.py:17
  126.7 1.8 %collective-permute-done.6 = bf16[4,16,1,320]{3,1,2,0:T(8,128)(2,1)S(1)} collective-permute-done((bf16[4,16,1,320]{3,1,2,0:T(8,128)(2,1)S(1)}, bf16[4,16,1,320]{3,1,2,0:T(8,128)(2,1)S(1)}, u32[]{:S(2)}, u32[]{:S(2)}) %collective-permute-start.6) | collective-permute-done | bytes 40992 | tf_op jit(solution)/shard_map/ppermute | solution.py:16
  128.5 0.2 pad_maximum_fusion.2
  128.7 2.3 %collective-permute-start.10 = (bf16[4,18,320]{2,0,1:T(4,128)(2,1)S(1)}, bf16[4,18,320]{2,0,1:T(4,128)(2,1)S(1)}, u32[]{:S(2)}, u32[]{:S(2)}) collective-permute-start(bf16[4,18,320]{2,0,1:T(4,128)(2,1)S(1)} %bitcast.77), channel_id=1, source_target_pairs={{0,16},{4,20},{8,24},{12,28},{16,0},{20,4},{24,8},{28,12},{1,17},{... | collective-permute-start | bytes 138248 | tf_op jit(solution)/shard_map/ppermute | solution.py:24
  131.1 1.3 collective-permute-start.11
  132.4 4.6 %collective-permute-start.9 = (bf16[4,1,18,320]{3,1,2,0:T(2,128)(2,1)S(1)}, bf16[4,1,18,320]{3,1,2,0:T(2,128)(2,1)S(1)}, u32[]{:S(2)}, u32[]{:S(2)}) collective-permute-start(bf16[4,1,18,320]{3,1,2,0:T(2,128)(2,1)S(1)} %get-tuple-element.12), channel_id=1, source_target_pairs={{0,1},{1,2},{2,3},{4,5},{5,6},{6,7},{8,9},{9,10},{10,11},{12,13},{... | collective-permute-start | bytes 138248 | tf_op jit(solution)/shard_map/ppermute | solution.py:16
  137.0 0.1 collective-permute-start.8
  137.1 0.6 collective-permute-done.11
  137.8 0.1 copy.129
  137.9 3.3 %collective-permute-done.8 = bf16[4,18,320]{2,0,1:T(4,128)(2,1)S(1)} collective-permute-done((bf16[4,18,320]{2,0,1:T(4,128)(2,1)S(1)}, bf16[4,18,320]{2,0,1:T(4,128)(2,1)S(1)}, u32[]{:S(2)}, u32[]{:S(2)}) %collective-permute-start.8) | collective-permute-done | bytes 46112 | tf_op jit(solution)/shard_map/ppermute | solution.py:24
  141.2 0.1 copy.128
  141.3 0.9 maximum_bitcast_fusion
  142.2 0.4 copy.136
  142.6 0.5 pad.2.clone
  143.1 0.3 slice.50
  143.4 1.0 fusion.6
  144.5 0.5 copy-done.6
  145.0 5.0 %select_add_fusion = f32[16,32,3,320]{3,1,2,0:T(8,128)S(1)} fusion(bf16[3,3,320,320]{3,2,1,0:T(8,128)(2,1)S(1)} %copy-done.6, bf16[18,4,8,5,320]{4,1,3,2,0:T(4,128)(2,1)S(1)} %fusion.6, f32[320]{0:T(512)S(1)} %copy-done.8, pred[32,3]{0,1:T(4,128)(4,1)S(1)} %copy-done.9), kind=kOutput, calls=%fused_computation.13 | convolution fusion | flops 2832138240 | bytes 5653856 | tf_op jit(solution)/shard_map/conv_general_dilated | solution.py:65
  150.0 1.4 copy.132
  151.4 0.1 slice.51
  151.5 1.0 copy-done.2
  152.5 1.4 fusion.17
  154.0 1.0 copy.134
  (39 shorter events, 0.8 us)
Async XLA Ops:
  0.0 67.6 %copy-start = (bf16[3,3,320,320]{3,2,1,0:T(8,128)(2,1)S(1)}, bf16[3,3,320,320]{3,2,1,0:T(8,128)(2,1)}, u32[]{:S(2)}) copy-start(bf16[3,3,320,320]{3,2,1,0:T(8,128)(2,1)} %param.13) | copy-start | bytes 5529604
  47.4 4.5 %collective-permute-start = (bf16[4,16,1,320]{3,0,2,1:T(4,128)(2,1)S(1)}, bf16[4,16,1,320]{3,0,2,1:T(4,128)(2,1)S(1)}, u32[]{:S(2)}, u32[]{:S(2)}) collective-permute-start(bf16[4,16,1,320]{3,0,2,1:T(4,128)(2,1)S(1)} %get-tuple-element.17), channel_id=1, source_target_pairs={{0,4},{4,8},{8,12},{12,16},{16,20},{20,24},{24,28},{28,0},{1,5},{5... | collective-permute-start | bytes 122888 | tf_op jit(solution)/shard_map/ppermute | solution.py:16
  47.5 4.4 %collective-permute-start.1 = (bf16[4,16,1,320]{3,0,2,1:T(4,128)(2,1)S(1)}, bf16[4,16,1,320]{3,0,2,1:T(4,128)(2,1)S(1)}, u32[]{:S(2)}, u32[]{:S(2)}) collective-permute-start(bf16[4,16,1,320]{3,0,2,1:T(4,128)(2,1)S(1)} %get-tuple-element.18), channel_id=1, source_target_pairs={{4,0},{8,4},{12,8},{16,12},{20,16},{24,20},{28,24},{0,28},{5,1},{9... | collective-permute-start | bytes 122888 | tf_op jit(solution)/shard_map/ppermute | solution.py:17
  52.0 8.5 %collective-permute-start.4 = (bf16[4,18,320]{2,0,1:T(4,128)(2,1)S(1)}, bf16[4,18,320]{2,0,1:T(4,128)(2,1)S(1)}, u32[]{:S(2)}, u32[]{:S(2)}) collective-permute-start(bf16[4,18,320]{2,0,1:T(4,128)(2,1)S(1)} %bitcast.78), channel_id=1, source_target_pairs={{0,16},{4,20},{8,24},{12,28},{16,0},{20,4},{24,8},{28,12},{1,17},{... | collective-permute-start | bytes 138248 | tf_op jit(solution)/shard_map/ppermute | solution.py:24
  54.3 6.1 %collective-permute-start.5 = (bf16[4,1,18,320]{3,0,2,1:T(4,128)(2,1)S(1)}, bf16[4,1,18,320]{3,0,2,1:T(4,128)(2,1)S(1)}, u32[]{:S(2)}, u32[]{:S(2)}) collective-permute-start(bf16[4,1,18,320]{3,0,2,1:T(4,128)(2,1)S(1)} %get-tuple-element.13), channel_id=1, source_target_pairs={{1,0},{2,1},{3,2},{5,4},{6,5},{7,6},{9,8},{10,9},{11,10},{13,12},{... | collective-permute-start | bytes 138248 | tf_op jit(solution)/shard_map/ppermute | solution.py:17
  55.6 9.0 %collective-permute-start.3 = (bf16[4,1,18,320]{3,0,2,1:T(4,128)(2,1)S(1)}, bf16[4,1,18,320]{3,0,2,1:T(4,128)(2,1)S(1)}, u32[]{:S(2)}, u32[]{:S(2)}) collective-permute-start(bf16[4,1,18,320]{3,0,2,1:T(4,128)(2,1)S(1)} %get-tuple-element.14), channel_id=1, source_target_pairs={{0,1},{1,2},{2,3},{4,5},{5,6},{6,7},{8,9},{9,10},{10,11},{12,13},{... | collective-permute-start | bytes 138248 | tf_op jit(solution)/shard_map/ppermute | solution.py:16
  60.4 4.2 %collective-permute-start.2 = (bf16[4,18,320]{2,0,1:T(4,128)(2,1)S(1)}, bf16[4,18,320]{2,0,1:T(4,128)(2,1)S(1)}, u32[]{:S(2)}, u32[]{:S(2)}) collective-permute-start(bf16[4,18,320]{2,0,1:T(4,128)(2,1)S(1)} %bitcast.79), channel_id=1, source_target_pairs={{0,16},{4,20},{8,24},{12,28},{16,0},{20,4},{24,8},{28,12},{1,17},{... | collective-permute-start | bytes 138248 | tf_op jit(solution)/shard_map/ppermute | solution.py:24
  66.4 1.1 copy-start.3
  67.4 0.7 copy-start.7
  67.4 0.7 copy-start.9
  120.1 1.7 %copy-start.1 = (f32[16,32,3,320]{3,1,2,0:T(8,128)S(1)}, f32[16,32,3,320]{3,1,2,0:T(8,128)}, u32[]{:S(2)}) copy-start(f32[16,32,3,320]{3,1,2,0:T(8,128)} %get-tuple-element.24) | copy-start | bytes 5898244
  120.1 1.7 %copy-start.4 = (f32[320]{0:T(512)S(1)}, f32[320]{0:T(512)}, u32[]{:S(2)}) copy-start(f32[320]{0:T(512)} %param.17) | copy-start | bytes 3844
  120.1 1.7 %copy-start.5 = (f32[320]{0:T(512)S(1)}, f32[320]{0:T(512)}, u32[]{:S(2)}) copy-start(f32[320]{0:T(512)} %param.16) | copy-start | bytes 3844
  124.0 4.5 %collective-permute-start.6 = (bf16[4,16,1,320]{3,1,2,0:T(8,128)(2,1)S(1)}, bf16[4,16,1,320]{3,1,2,0:T(8,128)(2,1)S(1)}, u32[]{:S(2)}, u32[]{:S(2)}) collective-permute-start(bf16[4,16,1,320]{3,1,2,0:T(8,128)(2,1)S(1)} %get-tuple-element.15), channel_id=1, source_target_pairs={{0,4},{4,8},{8,12},{12,16},{16,20},{20,24},{24,28},{28,0},{1,5},{5... | collective-permute-start | bytes 122888 | tf_op jit(solution)/shard_map/ppermute | solution.py:16
  124.1 4.4 %collective-permute-start.7 = (bf16[4,16,1,320]{3,1,2,0:T(8,128)(2,1)S(1)}, bf16[4,16,1,320]{3,1,2,0:T(8,128)(2,1)S(1)}, u32[]{:S(2)}, u32[]{:S(2)}) collective-permute-start(bf16[4,16,1,320]{3,1,2,0:T(8,128)(2,1)S(1)} %get-tuple-element.16), channel_id=1, source_target_pairs={{4,0},{8,4},{12,8},{16,12},{20,16},{24,20},{28,24},{0,28},{5,1},{9... | collective-permute-start | bytes 122888 | tf_op jit(solution)/shard_map/ppermute | solution.py:17
  128.7 8.3 %collective-permute-start.10 = (bf16[4,18,320]{2,0,1:T(4,128)(2,1)S(1)}, bf16[4,18,320]{2,0,1:T(4,128)(2,1)S(1)}, u32[]{:S(2)}, u32[]{:S(2)}) collective-permute-start(bf16[4,18,320]{2,0,1:T(4,128)(2,1)S(1)} %bitcast.77), channel_id=1, source_target_pairs={{0,16},{4,20},{8,24},{12,28},{16,0},{20,4},{24,8},{28,12},{1,17},{... | collective-permute-start | bytes 138248 | tf_op jit(solution)/shard_map/ppermute | solution.py:24
  131.1 6.6 %collective-permute-start.11 = (bf16[4,1,18,320]{3,1,2,0:T(2,128)(2,1)S(1)}, bf16[4,1,18,320]{3,1,2,0:T(2,128)(2,1)S(1)}, u32[]{:S(2)}, u32[]{:S(2)}) collective-permute-start(bf16[4,1,18,320]{3,1,2,0:T(2,128)(2,1)S(1)} %get-tuple-element.11), channel_id=1, source_target_pairs={{1,0},{2,1},{3,2},{5,4},{6,5},{7,6},{9,8},{10,9},{11,10},{13,12},{... | collective-permute-start | bytes 138248 | tf_op jit(solution)/shard_map/ppermute | solution.py:17
  132.4 8.8 %collective-permute-start.9 = (bf16[4,1,18,320]{3,1,2,0:T(2,128)(2,1)S(1)}, bf16[4,1,18,320]{3,1,2,0:T(2,128)(2,1)S(1)}, u32[]{:S(2)}, u32[]{:S(2)}) collective-permute-start(bf16[4,1,18,320]{3,1,2,0:T(2,128)(2,1)S(1)} %get-tuple-element.12), channel_id=1, source_target_pairs={{0,1},{1,2},{2,3},{4,5},{5,6},{6,7},{8,9},{9,10},{10,11},{12,13},{... | collective-permute-start | bytes 138248 | tf_op jit(solution)/shard_map/ppermute | solution.py:16
  137.0 4.2 %collective-permute-start.8 = (bf16[4,18,320]{2,0,1:T(4,128)(2,1)S(1)}, bf16[4,18,320]{2,0,1:T(4,128)(2,1)S(1)}, u32[]{:S(2)}, u32[]{:S(2)}) collective-permute-start(bf16[4,18,320]{2,0,1:T(4,128)(2,1)S(1)} %bitcast.76), channel_id=1, source_target_pairs={{0,16},{4,20},{8,24},{12,28},{16,0},{20,4},{24,8},{28,12},{1,17},{... | collective-permute-start | bytes 138248 | tf_op jit(solution)/shard_map/ppermute | solution.py:24
  143.4 1.6 %copy-start.6 = (bf16[3,3,320,320]{3,2,1,0:T(8,128)(2,1)S(1)}, bf16[3,3,320,320]{3,2,1,0:T(8,128)(2,1)}, u32[]{:S(2)}) copy-start(bf16[3,3,320,320]{3,2,1,0:T(8,128)(2,1)} %param.18) | copy-start | bytes 5529604
  143.4 1.6 %copy-start.8 = (f32[320]{0:T(512)S(1)}, f32[320]{0:T(512)}, u32[]{:S(2)}) copy-start(f32[320]{0:T(512)} %param.19) | copy-start | bytes 3844
  151.4 1.1 copy-start.2
where the time goes:
time: 156 us; the launch traced here: 155 us
  blocking collectives  81.4 us (52%)
  starting transfers between devices  22.1 us (14%)
  local copies, waits for them, and re-layouts  14.6 us (9%)
  other arithmetic  12.7 us (8%)
  matrix products  12.1 us (8%)
  waiting for transfers between devices  11.6 us (7%)
    psum x2, blocking collectives, group_stats(): lax.psum((jnp.sum(grouped, axis=(1, 3)), jnp.sum(grouped * grouped, axis=...  81.4 us
    conv_general_dilated x2, matrix products, convolve(): lax.conv_general_dilated(padded, weight, (1, 1), 'VALID', dimension_numbe...  12.1 us
    ppermute x4, starting transfers between devices, padded_2(): before = lax.ppermute(last, axis, up)  9.4 us
    ppermute x4, starting transfers between devices, padded_2(): after = lax.ppermute(leading, axis, down)  7.82 us
    ppermute x4, waiting for transfers between devices, from_behind(): lax.ppermute(array, axis, [(i, (i + by) % devices) for i in range(devices)])  7.42 us
    ppermute x4, starting transfers between devices, from_behind(): lax.ppermute(array, axis, [(i, (i + by) % devices) for i in range(devices)])  4.85 us
    convert_element_type x2, other arithmetic, activate(): return jax.nn.silu(normed).astype(jnp.bfloat16)  4.24 us
    unnamed x21, local copies, waits for them, and re-layouts  3.76 us
  transfers between devices with their start and end apart: 12, of which 5 were waited for; matrix products, arithmetic and copies ran while one was open for 0% of the time, Pallas kernels for 0%

commit v1 on v0

--- a/solution.py
+++ b/solution.py
@@ -25,10 +25,16 @@
 
 
 def group_stats(field, cell_count):
+
+    def set_regions(x_in, dev_axis, bus_axis):
+        prior = jax.lax.psum(x_in, axis_name=dev_axis)
+        y = jax.lax.psum(prior, axis_name=bus_axis)
+        return y
+
     frame_count = field.shape[0]
     grouped = field.reshape(frame_count, -1, GROUPS, field.shape[3] // GROUPS)
-    summed, squares = lax.psum(
-        (jnp.sum(grouped, axis=(1, 3)), jnp.sum(grouped * grouped, axis=(1, 3))), ("lon", "lat")
+    summed, squares = set_regions(
+        (jnp.sum(grouped, axis=(1, 3)), jnp.sum(grouped * grouped, axis=(1, 3))), "lat", "lon"
     )
     average = summed / cell_count
     variance = squares / cell_count - average * average

time: 156 us -> 118 us (0.76)
  blocking collectives: 81.4 us -> 45.7 us
    psum x2 -> x4, blocking collectives: 81.4 us -> 45.7 us  [the longest x2 23.8 us: set_regions(): y = jax.lax.psum(prior, axis_name=bus_axis)]
  transfers between devices with their start and end apart: 12 -> 12, of which waited for: 5 -> 4; matrix products, arithmetic and copies ran while one was open for 0% -> 0% of each run, Pallas kernels for 0% -> 0%
where the time goes in v1:
time: 118 us; the launch traced here: 117 us
  blocking collectives  45.7 us (39%)
  starting transfers between devices  21.5 us (18%)
  local copies, waits for them, and re-layouts  14.6 us (12%)
  other arithmetic  12.7 us (11%)
  matrix products  12.1 us (10%)
  waiting for transfers between devices  10.4 us (9%)
    psum x2, blocking collectives, set_regions(): y = jax.lax.psum(prior, axis_name=bus_axis)  23.8 us
    psum x2, blocking collectives, set_regions(): prior = jax.lax.psum(x_in, axis_name=dev_axis)  21.9 us
    conv_general_dilated x2, matrix products, convolve(): lax.conv_general_dilated(padded, weight, (1, 1), 'VALID', dimension_numbe...  12.1 us
    ppermute x4, starting transfers between devices, padded_2(): before = lax.ppermute(last, axis, up)  9.4 us
    ppermute x4, starting transfers between devices, padded_2(): after = lax.ppermute(leading, axis, down)  7.82 us
    ppermute x4, waiting for transfers between devices, from_behind(): lax.ppermute(array, axis, [(i, (i + by) % devices) for i in range(devices)])  6.36 us
    ppermute x4, starting transfers between devices, from_behind(): lax.ppermute(array, axis, [(i, (i + by) % devices) for i in range(devices)])  4.31 us
    convert_element_type x2, other arithmetic, activate(): return jax.nn.silu(normed).astype(jnp.bfloat16)  4.24 us
  transfers between devices with their start and end apart: 12, of which 4 were waited for; matrix products, arithmetic and copies ran while one was open for 0% of the time, Pallas kernels for 0%

profile of v1, /device:TPU:0, one launch (start us, length us, event | category | flops | bytes accessed | tf_op | source)
XLA Modules:
  0.0 117.4 jit_solution(14688770237298395738)
XLA Ops:
  0.0 2.1 %convert_reduce_fusion = (f32[4,320]{1,0:T(4,128)S(1)}, f32[4,320]{1,0:T(4,128)S(1)}) fusion(bf16[4,16,16,320]{3,2,1,0:T(8,128)(2,1)} %param.10), kind=kLoop, calls=%fused_computation.6 | loop fusion | flops 1308160 | bytes 665600 | tf_op jit(solution)/shard_map/reduce_sum | solution.py:37
  2.1 0.1 reduce_sum.47
  2.2 0.1 reduce_sum.53
  2.4 0.1 reduce_sum.51
  2.5 0.1 reduce_sum.54
  2.6 13.5 %all-reduce.3 = (f32[4,32]{1,0:T(4,128)S(1)}, f32[4,32]{1,0:T(4,128)S(1)}) all-reduce(f32[4,32]{1,0:T(4,128)S(1)} %reduce_sum.54, f32[4,32]{1,0:T(4,128)S(1)} %reduce_sum.51), channel_id=1, replica_groups=mesh['lon'=8,'lat'=4] {'lat'}, use_global_device_ids=true, to_apply=%region_6.7 | all-reduce | flops 256 | bytes 2048 | tf_op jit(solution)/shard_map/psum | solution.py:30
  16.0 11.8 %all-reduce.1 = (f32[4,32]{1,0:T(4,128)S(1)}, f32[4,32]{1,0:T(4,128)S(1)}) all-reduce(f32[4,32]{1,0:T(4,128)S(1)} %get-tuple-element.13, f32[4,32]{1,0:T(4,128)S(1)} %get-tuple-element.14), channel_id=1, replica_groups=mesh['lon'=8,'lat'=4] {'lon'}, use_global_device_ids=true, to_apply=%region_7.8 | all-reduce | flops 256 | bytes 2048 | tf_op jit(solution)/shard_map/psum | solution.py:31
  27.9 0.1 sub.26
  28.1 0.1 mul.59
  28.3 2.4 %fusion.18 = bf16[4,16,16,320]{3,0,2,1:T(4,128)(2,1)S(1)} fusion(f32[320]{0:T(512)} %param.12, f32[320]{0:T(512)} %param.11, f32[4,320]{1,0:T(4,128)S(1)} %mul.59, f32[4,320]{1,0:T(4,128)S(1)} %sub.26, bf16[4,16,16,320]{3,2,1,0:T(8,128)(2,1)} %param.10), kind=kLoop, calls=%fused_computation.32 | loop fusion | flops 3276800 | bytes 1323520 | tf_op jit(solution)/shard_map/convert_element_type | solution.py:49
  30.8 2.6 %collective-permute-start.1 = (bf16[4,16,1,320]{3,0,2,1:T(4,128)(2,1)S(1)}, bf16[4,16,1,320]{3,0,2,1:T(4,128)(2,1)S(1)}, u32[]{:S(2)}, u32[]{:S(2)}) collective-permute-start(bf16[4,16,1,320]{3,0,2,1:T(4,128)(2,1)S(1)} %get-tuple-element.22), channel_id=1, source_target_pairs={{4,0},{8,4},{12,8},{16,12},{20,16},{24,20},{28,24},{0,28},{5,1},{9... | collective-permute-start | bytes 122888 | tf_op jit(solution)/shard_map/ppermute | solution.py:17
  33.5 2.2 %collective-permute-done = bf16[4,16,1,320]{3,0,2,1:T(4,128)(2,1)S(1)} collective-permute-done((bf16[4,16,1,320]{3,0,2,1:T(4,128)(2,1)S(1)}, bf16[4,16,1,320]{3,0,2,1:T(4,128)(2,1)S(1)}, u32[]{:S(2)}, u32[]{:S(2)}) %collective-permute-start) | collective-permute-done | bytes 40992 | tf_op jit(solution)/shard_map/ppermute | solution.py:16
  35.6 0.1 pad_maximum_fusion.5
  35.7 1.2 %collective-permute-start.4 = (bf16[4,18,320]{2,0,1:T(4,128)(2,1)S(1)}, bf16[4,18,320]{2,0,1:T(4,128)(2,1)S(1)}, u32[]{:S(2)}, u32[]{:S(2)}) collective-permute-start(bf16[4,18,320]{2,0,1:T(4,128)(2,1)S(1)} %bitcast.78), channel_id=1, source_target_pairs={{0,16},{4,20},{8,24},{12,28},{16,0},{20,4},{24,8},{28,12},{1,17},{... | collective-permute-start | bytes 138248 | tf_op jit(solution)/shard_map/ppermute | solution.py:24
  36.9 1.3 %collective-permute-start.5 = (bf16[4,1,18,320]{3,0,2,1:T(4,128)(2,1)S(1)}, bf16[4,1,18,320]{3,0,2,1:T(4,128)(2,1)S(1)}, u32[]{:S(2)}, u32[]{:S(2)}) collective-permute-start(bf16[4,1,18,320]{3,0,2,1:T(4,128)(2,1)S(1)} %get-tuple-element.17), channel_id=1, source_target_pairs={{1,0},{2,1},{3,2},{5,4},{6,5},{7,6},{9,8},{10,9},{11,10},{13,12},{... | collective-permute-start | bytes 138248 | tf_op jit(solution)/shard_map/ppermute | solution.py:17
  38.2 4.7 %collective-permute-start.3 = (bf16[4,1,18,320]{3,0,2,1:T(4,128)(2,1)S(1)}, bf16[4,1,18,320]{3,0,2,1:T(4,128)(2,1)S(1)}, u32[]{:S(2)}, u32[]{:S(2)}) collective-permute-start(bf16[4,1,18,320]{3,0,2,1:T(4,128)(2,1)S(1)} %get-tuple-element.18), channel_id=1, source_target_pairs={{0,1},{1,2},{2,3},{4,5},{5,6},{6,7},{8,9},{9,10},{10,11},{12,13},{... | collective-permute-start | bytes 138248 | tf_op jit(solution)/shard_map/ppermute | solution.py:16
  43.0 0.9 collective-permute-start.2
  43.9 3.2 %collective-permute-done.2 = bf16[4,18,320]{2,0,1:T(4,128)(2,1)S(1)} collective-permute-done((bf16[4,18,320]{2,0,1:T(4,128)(2,1)S(1)}, bf16[4,18,320]{2,0,1:T(4,128)(2,1)S(1)}, u32[]{:S(2)}, u32[]{:S(2)}) %collective-permute-start.2) | collective-permute-done | bytes 46112 | tf_op jit(solution)/shard_map/ppermute | solution.py:24
  47.2 0.9 maximum_bitcast_fusion.1
  48.1 0.5 pad
  48.6 0.3 slice.44
  48.9 1.0 fusion.5
  50.0 0.2 broadcast.25
  50.2 0.5 copy-done.7
  50.7 7.1 %fusion.30 = (f32[16,32,3,320]{3,1,2,0:T(8,128)S(1)}, f32[16,32,3,320]{3,1,2,0:T(8,128)}) fusion(f32[16,32,3,320]{3,0,2,1:T(8,128)S(1)} %bitcast.75, f32[320]{0:T(512)S(1)} %copy-done.7, bf16[3,3,320,320]{3,2,1,0:T(8,128)(2,1)S(1)} %copy-done, bf16[18,4,8,5,320]{4,1,3,2,0:T(4,128)(2,1)S(1)} %fusion.5, pred[32,3]{0,1:T(4,128)(4,1)S(1)} %copy-done.9), kind=kOutput, calls=%fused_computation.59 | convolution fusion | flops 2834104320 | bytes 9586016 | tf_op jit(solution)/shard_map/conv_general_dilated | solution.py:71
  57.7 1.4 %copy.121 = f32[16,32,3,320]{3,0,2,1:T(8,128)S(1)} copy(f32[16,32,3,320]{3,1,2,0:T(8,128)S(1)} %get-tuple-element.27) | data formatting | bytes 3932160 | tf_op jit(solution)/shard_map/mul | solution.py:37
  59.1 0.1 slice_reduce_fusion
  59.2 0.1 reduce_sum.74
  59.3 0.1 reduce_sum.75
  59.4 3.0 %copy.119 = f32[16,32,3,320]{3,0,2,1:T(8,128)S(1)} copy(f32[16,32,3,320]{3,1,2,0:T(8,128)} %get-tuple-element.28) | data formatting | bytes 3932160 | tf_op jit(solution)/shard_map/convert_element_type | solution.py:65
  62.5 0.1 slice_reduce_fusion.1
  62.6 0.1 reduce_sum.59
  62.7 0.1 reduce_sum.72
  62.8 8.4 %all-reduce.2 = (f32[4,32]{1,0:T(4,128)S(1)}, f32[4,32]{1,0:T(4,128)S(1)}) all-reduce(f32[4,32]{1,0:T(4,128)S(1)} %reduce_sum.75, f32[4,32]{1,0:T(4,128)S(1)} %reduce_sum.72), channel_id=1, replica_groups=mesh['lon'=8,'lat'=4] {'lat'}, use_global_device_ids=true, to_apply=%region_14.15 | all-reduce | flops 256 | bytes 2048 | tf_op jit(solution)/shard_map/psum | solution.py:30
  71.2 12.0 %all-reduce = (f32[4,32]{1,0:T(4,128)S(1)}, f32[4,32]{1,0:T(4,128)S(1)}) all-reduce(f32[4,32]{1,0:T(4,128)S(1)} %get-tuple-element.11, f32[4,32]{1,0:T(4,128)S(1)} %get-tuple-element.12), channel_id=1, replica_groups=mesh['lon'=8,'lat'=4] {'lon'}, use_global_device_ids=true, to_apply=%region_15.16 | all-reduce | flops 256 | bytes 2048 | tf_op jit(solution)/shard_map/psum | solution.py:31
  83.3 0.1 sub.30
  83.5 0.1 mul.67
  83.6 0.2 broadcast.27
  83.8 0.2 broadcast.26
  84.0 1.3 %copy-done.1 = f32[16,32,3,320]{3,1,2,0:T(8,128)S(1)} copy-done((f32[16,32,3,320]{3,1,2,0:T(8,128)S(1)}, f32[16,32,3,320]{3,1,2,0:T(8,128)}, u32[]{:S(2)}) %copy-start.1) | copy-done | bytes 1966104
  85.3 1.8 %multiply_convert_fusion = bf16[16,32,3,320]{3,1,2,0:T(8,128)(2,1)S(1)} fusion(f32[16,32,3,320]{3,0,2,1:T(8,128)S(1)} %bitcast.65, f32[16,32,3,320]{3,1,2,0:T(8,128)S(1)} %copy-done.1, f32[16,32,3,320]{3,0,2,1:T(8,128)S(1)} %bitcast.66, f32[320]{0:T(512)S(1)} %copy-done.4, f32[320]{0:T(512)S(1)} %copy-done.5), kind=kLoop, calls=%fused_computation.14 | loop fusion | flops 4423680 | bytes 6883840 | tf_op jit(solution)/shard_map/convert_element_type | solution.py:49
  87.1 0.4 copy.123
  87.6 2.6 %collective-permute-start.7 = (bf16[4,16,1,320]{3,1,2,0:T(8,128)(2,1)S(1)}, bf16[4,16,1,320]{3,1,2,0:T(8,128)(2,1)S(1)}, u32[]{:S(2)}, u32[]{:S(2)}) collective-permute-start(bf16[4,16,1,320]{3,1,2,0:T(8,128)(2,1)S(1)} %get-tuple-element.20), channel_id=1, source_target_pairs={{4,0},{8,4},{12,8},{16,12},{20,16},{24,20},{28,24},{0,28},{5,1},{9... | collective-permute-start | bytes 122888 | tf_op jit(solution)/shard_map/ppermute | solution.py:17
  90.3 1.8 %collective-permute-done.6 = bf16[4,16,1,320]{3,1,2,0:T(8,128)(2,1)S(1)} collective-permute-done((bf16[4,16,1,320]{3,1,2,0:T(8,128)(2,1)S(1)}, bf16[4,16,1,320]{3,1,2,0:T(8,128)(2,1)S(1)}, u32[]{:S(2)}, u32[]{:S(2)}) %collective-permute-start.6) | collective-permute-done | bytes 40992 | tf_op jit(solution)/shard_map/ppermute | solution.py:16
  92.1 0.2 pad_maximum_fusion.2
  92.3 1.2 %collective-permute-start.10 = (bf16[4,18,320]{2,0,1:T(4,128)(2,1)S(1)}, bf16[4,18,320]{2,0,1:T(4,128)(2,1)S(1)}, u32[]{:S(2)}, u32[]{:S(2)}) collective-permute-start(bf16[4,18,320]{2,0,1:T(4,128)(2,1)S(1)} %bitcast.77), channel_id=1, source_target_pairs={{0,16},{4,20},{8,24},{12,28},{16,0},{20,4},{24,8},{28,12},{1,17},{... | collective-permute-start | bytes 138248 | tf_op jit(solution)/shard_map/ppermute | solution.py:24
  93.6 1.3 %collective-permute-start.11 = (bf16[4,1,18,320]{3,1,2,0:T(2,128)(2,1)S(1)}, bf16[4,1,18,320]{3,1,2,0:T(2,128)(2,1)S(1)}, u32[]{:S(2)}, u32[]{:S(2)}) collective-permute-start(bf16[4,1,18,320]{3,1,2,0:T(2,128)(2,1)S(1)} %get-tuple-element.15), channel_id=1, source_target_pairs={{1,0},{2,1},{3,2},{5,4},{6,5},{7,6},{9,8},{10,9},{11,10},{13,12},{... | collective-permute-start | bytes 138248 | tf_op jit(solution)/shard_map/ppermute | solution.py:17
  94.9 4.6 %collective-permute-start.9 = (bf16[4,1,18,320]{3,1,2,0:T(2,128)(2,1)S(1)}, bf16[4,1,18,320]{3,1,2,0:T(2,128)(2,1)S(1)}, u32[]{:S(2)}, u32[]{:S(2)}) collective-permute-start(bf16[4,1,18,320]{3,1,2,0:T(2,128)(2,1)S(1)} %get-tuple-element.16), channel_id=1, source_target_pairs={{0,1},{1,2},{2,3},{4,5},{5,6},{6,7},{8,9},{9,10},{10,11},{12,13},{... | collective-permute-start | bytes 138248 | tf_op jit(solution)/shard_map/ppermute | solution.py:16
  99.4 0.9 collective-permute-start.8
  100.4 0.1 copy.129
  100.5 3.1 %collective-permute-done.8 = bf16[4,18,320]{2,0,1:T(4,128)(2,1)S(1)} collective-permute-done((bf16[4,18,320]{2,0,1:T(4,128)(2,1)S(1)}, bf16[4,18,320]{2,0,1:T(4,128)(2,1)S(1)}, u32[]{:S(2)}, u32[]{:S(2)}) %collective-permute-start.8) | collective-permute-done | bytes 46112 | tf_op jit(solution)/shard_map/ppermute | solution.py:24
  103.7 0.1 copy.128
  103.8 0.9 maximum_bitcast_fusion
  104.7 0.4 copy.136
  105.1 0.5 pad.2.clone
  105.6 0.3 slice.50
  105.9 1.0 fusion.6
  106.9 0.5 copy-done.6
  107.5 5.0 %select_add_fusion = f32[16,32,3,320]{3,1,2,0:T(8,128)S(1)} fusion(bf16[3,3,320,320]{3,2,1,0:T(8,128)(2,1)S(1)} %copy-done.6, bf16[18,4,8,5,320]{4,1,3,2,0:T(4,128)(2,1)S(1)} %fusion.6, f32[320]{0:T(512)S(1)} %copy-done.8, pred[32,3]{0,1:T(4,128)(4,1)S(1)} %copy-done.9), kind=kOutput, calls=%fused_computation.13 | convolution fusion | flops 2832138240 | bytes 5653856 | tf_op jit(solution)/shard_map/conv_general_dilated | solution.py:71
  112.5 1.4 %copy.132 = f32[16,32,3,320]{3,0,2,1:T(8,128)S(1)} copy(f32[16,32,3,320]{3,1,2,0:T(8,128)S(1)} %select_add_fusion) | data formatting | bytes 3932160 | tf_op jit(solution)/shard_map/add | solution.py:101
  113.9 0.1 slice.51
  114.0 1.0 copy-done.2
  115.0 1.4 %fusion.17 = bf16[4,16,16,320]{3,0,2,1:T(4,128)(2,1)S(1)} fusion(f32[16,4,16,320]{3,0,2,1:T(8,128)S(1)} %slice.51, bf16[4,16,16,320]{3,2,1,0:T(8,128)(2,1)S(1)} %copy-done.2), kind=kLoop, calls=%fused_computation.28 | loop fusion | flops 983040 | bytes 2621440 | tf_op jit(solution)/shard_map/convert_element_type | solution.py:102
  116.4 1.0 copy.134
  (41 shorter events, 0.8 us)
Async XLA Ops:
  0.0 50.2 %copy-start = (bf16[3,3,320,320]{3,2,1,0:T(8,128)(2,1)S(1)}, bf16[3,3,320,320]{3,2,1,0:T(8,128)(2,1)}, u32[]{:S(2)}) copy-start(bf16[3,3,320,320]{3,2,1,0:T(8,128)(2,1)} %param.13) | copy-start | bytes 5529604
  30.8 4.9 %collective-permute-start = (bf16[4,16,1,320]{3,0,2,1:T(4,128)(2,1)S(1)}, bf16[4,16,1,320]{3,0,2,1:T(4,128)(2,1)S(1)}, u32[]{:S(2)}, u32[]{:S(2)}) collective-permute-start(bf16[4,16,1,320]{3,0,2,1:T(4,128)(2,1)S(1)} %get-tuple-element.21), channel_id=1, source_target_pairs={{0,4},{4,8},{8,12},{12,16},{16,20},{20,24},{24,28},{28,0},{1,5},{5... | collective-permute-start | bytes 122888 | tf_op jit(solution)/shard_map/ppermute | solution.py:16
  30.8 4.8 %collective-permute-start.1 = (bf16[4,16,1,320]{3,0,2,1:T(4,128)(2,1)S(1)}, bf16[4,16,1,320]{3,0,2,1:T(4,128)(2,1)S(1)}, u32[]{:S(2)}, u32[]{:S(2)}) collective-permute-start(bf16[4,16,1,320]{3,0,2,1:T(4,128)(2,1)S(1)} %get-tuple-element.22), channel_id=1, source_target_pairs={{4,0},{8,4},{12,8},{16,12},{20,16},{24,20},{28,24},{0,28},{5,1},{9... | collective-permute-start | bytes 122888 | tf_op jit(solution)/shard_map/ppermute | solution.py:17
  35.7 8.2 %collective-permute-start.4 = (bf16[4,18,320]{2,0,1:T(4,128)(2,1)S(1)}, bf16[4,18,320]{2,0,1:T(4,128)(2,1)S(1)}, u32[]{:S(2)}, u32[]{:S(2)}) collective-permute-start(bf16[4,18,320]{2,0,1:T(4,128)(2,1)S(1)} %bitcast.78), channel_id=1, source_target_pairs={{0,16},{4,20},{8,24},{12,28},{16,0},{20,4},{24,8},{28,12},{1,17},{... | collective-permute-start | bytes 138248 | tf_op jit(solution)/shard_map/ppermute | solution.py:24
  36.9 7.0 %collective-permute-start.5 = (bf16[4,1,18,320]{3,0,2,1:T(4,128)(2,1)S(1)}, bf16[4,1,18,320]{3,0,2,1:T(4,128)(2,1)S(1)}, u32[]{:S(2)}, u32[]{:S(2)}) collective-permute-start(bf16[4,1,18,320]{3,0,2,1:T(4,128)(2,1)S(1)} %get-tuple-element.17), channel_id=1, source_target_pairs={{1,0},{2,1},{3,2},{5,4},{6,5},{7,6},{9,8},{10,9},{11,10},{13,12},{... | collective-permute-start | bytes 138248 | tf_op jit(solution)/shard_map/ppermute | solution.py:17
  38.2 9.0 %collective-permute-start.3 = (bf16[4,1,18,320]{3,0,2,1:T(4,128)(2,1)S(1)}, bf16[4,1,18,320]{3,0,2,1:T(4,128)(2,1)S(1)}, u32[]{:S(2)}, u32[]{:S(2)}) collective-permute-start(bf16[4,1,18,320]{3,0,2,1:T(4,128)(2,1)S(1)} %get-tuple-element.18), channel_id=1, source_target_pairs={{0,1},{1,2},{2,3},{4,5},{5,6},{6,7},{8,9},{9,10},{10,11},{12,13},{... | collective-permute-start | bytes 138248 | tf_op jit(solution)/shard_map/ppermute | solution.py:16
  43.0 4.2 %collective-permute-start.2 = (bf16[4,18,320]{2,0,1:T(4,128)(2,1)S(1)}, bf16[4,18,320]{2,0,1:T(4,128)(2,1)S(1)}, u32[]{:S(2)}, u32[]{:S(2)}) collective-permute-start(bf16[4,18,320]{2,0,1:T(4,128)(2,1)S(1)} %bitcast.79), channel_id=1, source_target_pairs={{0,16},{4,20},{8,24},{12,28},{16,0},{20,4},{24,8},{28,12},{1,17},{... | collective-permute-start | bytes 138248 | tf_op jit(solution)/shard_map/ppermute | solution.py:24
  48.9 1.1 copy-start.3
  50.0 0.7 copy-start.7
  50.0 0.7 copy-start.9
  83.6 1.7 %copy-start.1 = (f32[16,32,3,320]{3,1,2,0:T(8,128)S(1)}, f32[16,32,3,320]{3,1,2,0:T(8,128)}, u32[]{:S(2)}) copy-start(f32[16,32,3,320]{3,1,2,0:T(8,128)} %get-tuple-element.28) | copy-start | bytes 5898244
  83.6 1.7 %copy-start.4 = (f32[320]{0:T(512)S(1)}, f32[320]{0:T(512)}, u32[]{:S(2)}) copy-start(f32[320]{0:T(512)} %param.17) | copy-start | bytes 3844
  83.6 1.7 %copy-start.5 = (f32[320]{0:T(512)S(1)}, f32[320]{0:T(512)}, u32[]{:S(2)}) copy-start(f32[320]{0:T(512)} %param.16) | copy-start | bytes 3844
  87.6 4.5 %collective-permute-start.6 = (bf16[4,16,1,320]{3,1,2,0:T(8,128)(2,1)S(1)}, bf16[4,16,1,320]{3,1,2,0:T(8,128)(2,1)S(1)}, u32[]{:S(2)}, u32[]{:S(2)}) collective-permute-start(bf16[4,16,1,320]{3,1,2,0:T(8,128)(2,1)S(1)} %get-tuple-element.19), channel_id=1, source_target_pairs={{0,4},{4,8},{8,12},{12,16},{16,20},{20,24},{24,28},{28,0},{1,5},{5... | collective-permute-start | bytes 122888 | tf_op jit(solution)/shard_map/ppermute | solution.py:16
  87.6 4.5 %collective-permute-start.7 = (bf16[4,16,1,320]{3,1,2,0:T(8,128)(2,1)S(1)}, bf16[4,16,1,320]{3,1,2,0:T(8,128)(2,1)S(1)}, u32[]{:S(2)}, u32[]{:S(2)}) collective-permute-start(bf16[4,16,1,320]{3,1,2,0:T(8,128)(2,1)S(1)} %get-tuple-element.20), channel_id=1, source_target_pairs={{4,0},{8,4},{12,8},{16,12},{20,16},{24,20},{28,24},{0,28},{5,1},{9... | collective-permute-start | bytes 122888 | tf_op jit(solution)/shard_map/ppermute | solution.py:17
  92.3 8.0 %collective-permute-start.10 = (bf16[4,18,320]{2,0,1:T(4,128)(2,1)S(1)}, bf16[4,18,320]{2,0,1:T(4,128)(2,1)S(1)}, u32[]{:S(2)}, u32[]{:S(2)}) collective-permute-start(bf16[4,18,320]{2,0,1:T(4,128)(2,1)S(1)} %bitcast.77), channel_id=1, source_target_pairs={{0,16},{4,20},{8,24},{12,28},{16,0},{20,4},{24,8},{28,12},{1,17},{... | collective-permute-start | bytes 138248 | tf_op jit(solution)/shard_map/ppermute | solution.py:24
  93.6 6.8 %collective-permute-start.11 = (bf16[4,1,18,320]{3,1,2,0:T(2,128)(2,1)S(1)}, bf16[4,1,18,320]{3,1,2,0:T(2,128)(2,1)S(1)}, u32[]{:S(2)}, u32[]{:S(2)}) collective-permute-start(bf16[4,1,18,320]{3,1,2,0:T(2,128)(2,1)S(1)} %get-tuple-element.15), channel_id=1, source_target_pairs={{1,0},{2,1},{3,2},{5,4},{6,5},{7,6},{9,8},{10,9},{11,10},{13,12},{... | collective-permute-start | bytes 138248 | tf_op jit(solution)/shard_map/ppermute | solution.py:17
  94.9 8.8 %collective-permute-start.9 = (bf16[4,1,18,320]{3,1,2,0:T(2,128)(2,1)S(1)}, bf16[4,1,18,320]{3,1,2,0:T(2,128)(2,1)S(1)}, u32[]{:S(2)}, u32[]{:S(2)}) collective-permute-start(bf16[4,1,18,320]{3,1,2,0:T(2,128)(2,1)S(1)} %get-tuple-element.16), channel_id=1, source_target_pairs={{0,1},{1,2},{2,3},{4,5},{5,6},{6,7},{8,9},{9,10},{10,11},{12,13},{... | collective-permute-start | bytes 138248 | tf_op jit(solution)/shard_map/ppermute | solution.py:16
  99.4 4.2 %collective-permute-start.8 = (bf16[4,18,320]{2,0,1:T(4,128)(2,1)S(1)}, bf16[4,18,320]{2,0,1:T(4,128)(2,1)S(1)}, u32[]{:S(2)}, u32[]{:S(2)}) collective-permute-start(bf16[4,18,320]{2,0,1:T(4,128)(2,1)S(1)} %bitcast.76), channel_id=1, source_target_pairs={{0,16},{4,20},{8,24},{12,28},{16,0},{20,4},{24,8},{28,12},{1,17},{... | collective-permute-start | bytes 138248 | tf_op jit(solution)/shard_map/ppermute | solution.py:24
  105.9 1.6 %copy-start.6 = (bf16[3,3,320,320]{3,2,1,0:T(8,128)(2,1)S(1)}, bf16[3,3,320,320]{3,2,1,0:T(8,128)(2,1)}, u32[]{:S(2)}) copy-start(bf16[3,3,320,320]{3,2,1,0:T(8,128)(2,1)} %param.18) | copy-start | bytes 5529604
  105.9 1.6 %copy-start.8 = (f32[320]{0:T(512)S(1)}, f32[320]{0:T(512)}, u32[]{:S(2)}) copy-start(f32[320]{0:T(512)} %param.19) | copy-start | bytes 3844
  113.9 1.1 copy-start.2
